TPU v7x, 32 devices: a whole 2x2x4 slice. The times are simulated.
32 devices in a mesh: groups: 2 (over x), ctx: 16 (over z, y, core).
Axes of the slice: x: 2, y: 2, z: 4, core: 2. Of those that a mesh axis runs over, the one named last changes fastest.
Arguments:
- hidden: bfloat16 [256, 8192], P('groups', 'ctx'), parts along dimension 0, may hold values from -6 to 6
- attn_gain: bfloat16 [8192], P('ctx'), may hold values from 0.25 to 1.75
- q_weight: bfloat16 [8192, 8192], P(None, 'ctx'), may hold values from -0.0625 to 0.0625
- q_gain: bfloat16 [128], replicated, may hold values from 0.25 to 1.75
- key_cache: bfloat16 [49152, 1024], P(('groups', 'ctx')), parts along dimension 0, may hold values from -64 to 64
- value_cache: bfloat16 [49152, 1024], P(('groups', 'ctx')), parts along dimension 0, may hold values from -6 to 6
- block_limit: int32 [256], P('groups'), parts along dimension 0, may hold values from 0 to 191, as said below
- out_weight: bfloat16 [8192, 8192], P('ctx'), may hold values from -0.09375 to 0.09375
- next_gain: bfloat16 [8192], P('ctx'), may hold values from 0.25 to 1.75
- next_weight: bfloat16 [8192, 8192], P(None, 'ctx'), may hold values from -0.0625 to 0.0625
Outputs:
- new_hidden: bfloat16 [256, 8192], P('groups', 'ctx'), parts along dimension 0
- next_queries: bfloat16 [256, 8192], P('groups', 'ctx'), parts along dimension 0
There are 2 independent parts, one for each index of `groups`. A program takes and returns all parts, laid end to end along the dimension named above; an argument that names none is the same for every part. Nothing has to cross between parts.
Inputs may be any that keep to these rules, and one draw needn't show every extreme that they name: Text token i may attend the visual blocks 0 to block_limit[i], each of 128 visual tokens; some token reaches the last block and some only the first.
All inputs are finite; a program needn't handle non-finite values.
Results may differ from a plain program's by a relative error of at most 0.015.
Values may be sent and summed in bfloat16 or wider, within the bound.
A program may use at most 64 MiB of HBM per device.

v0:
```python
import jax
import jax.numpy as jnp
from jax import lax
from jax.sharding import PartitionSpec as P

BLK = 128


EPSILON = 1e-05


def shifted(block, axis, distance):
    devices = range(lax.axis_size(axis))
    route = [((i - distance) % len(devices), i) for i in devices]
    return lax.ppermute(block, axis, route)


def normalize_project(share, gain_share, weight):
    whole, gains = (
        lax.all_gather(share, "ctx", axis=1, tiled=True),
        lax.all_gather(gain_share, "ctx", axis=0, tiled=True),
    )
    values = whole.astype(jnp.float32)
    factor = lax.rsqrt(jnp.mean(values * values, axis=1, keepdims=True) + EPSILON)
    normed = (values * factor * gains.astype(jnp.float32)).astype(jnp.bfloat16)
    return jnp.dot(normed, weight, preferred_element_type=jnp.float32)


def masked_scores(query_rows, keys, allowed, queries, heads_block, scale):
    scores = (
        lax.dot_general(
            query_rows, keys, (((1,), (1,)), ((), ())), preferred_element_type=jnp.float32
        )
        * scale
    )
    scores = scores.reshape(queries, heads_block, keys.shape[0])
    scores = jnp.where(allowed[:, None, :], scores, -jnp.inf)
    return scores.reshape(queries * heads_block, keys.shape[0])


def on_device(
    hidden,
    attn_gain,
    q_weight,
    q_gain,
    key_cache,
    value_cache,
    block_limit,
    out_weight,
    next_gain,
    next_weight,
):
    queries = hidden.shape[0]
    head_dim = q_gain.shape[0]
    devices = lax.axis_size("ctx")
    query = normalize_project(hidden, attn_gain, q_weight)
    heads_here = query.shape[1] // head_dim
    heads_total = heads_here * devices
    kv_heads = key_cache.shape[1] // head_dim
    group_size = heads_total // kv_heads
    shaped = query.reshape(queries, heads_here, head_dim)
    head_mean = jnp.mean(shaped * shaped, axis=-1, keepdims=True)
    query_normed = (shaped * lax.rsqrt(head_mean + EPSILON) * q_gain.astype(jnp.float32)).astype(
        jnp.bfloat16
    )
    local_tokens = key_cache.shape[0]
    device = lax.axis_index("ctx")
    blocks_here = (device * local_tokens + jnp.arange(local_tokens, dtype=jnp.int32)) // BLK
    allowed = blocks_here[None, :] <= block_limit[:, None]
    scale = head_dim ** (-0.5)
    count_rows = queries * heads_here

    def visit(step, carry):
        travelling, sums, peak, total = carry
        anchor = (device - step) % devices
        group = anchor * heads_here // group_size
        keys = lax.dynamic_slice_in_dim(key_cache, group * head_dim, head_dim, 1)
        values = lax.dynamic_slice_in_dim(value_cache, group * head_dim, head_dim, 1)
        scores = masked_scores(travelling, keys, allowed, queries, heads_here, scale)
        fresh = jnp.maximum(peak, jnp.max(scores, axis=1))
        expo = jnp.exp(scores - fresh[:, None])
        decay = jnp.exp(peak - fresh)
        total = total * decay + jnp.sum(expo, axis=1)
        sums = sums * decay[:, None] + jnp.dot(
            expo.astype(jnp.bfloat16), values, preferred_element_type=jnp.float32
        )
        travelling = shifted(travelling, "ctx", 1)
        sums, fresh, total = (
            shifted(sums.astype(jnp.bfloat16), "ctx", 1).astype(sums.dtype),
            shifted(fresh.astype(jnp.bfloat16), "ctx", 1).astype(fresh.dtype),
            shifted(total.astype(jnp.bfloat16), "ctx", 1).astype(total.dtype),
        )
        return (travelling, sums, fresh, total)

    start_state = (
        query_normed.reshape(count_rows, head_dim),
        jnp.zeros((count_rows, head_dim), jnp.float32),
        jnp.full((count_rows,), -1e30, jnp.float32),
        jnp.zeros((count_rows,), jnp.float32),
    )
    _, sums, peak, total = lax.fori_loop(0, devices, visit, start_state)
    attended = (sums / total[:, None]).astype(jnp.bfloat16).reshape(queries, heads_here * head_dim)
    mixed = lax.psum_scatter(
        lax.dot_general(
            out_weight, attended, (((0,), (1,)), ((), ())), preferred_element_type=jnp.float32
        ),
        "ctx",
        scatter_dimension=0,
        tiled=True,
    )
    new_hidden = (hidden.astype(jnp.float32) + mixed.T).astype(jnp.bfloat16)
    next_queries = normalize_project(new_hidden, next_gain, next_weight).astype(jnp.bfloat16)
    return (new_hidden, next_queries)


def solution(mesh):
    in_specs = (
        P("groups", "ctx"),
        P("ctx"),
        P(None, "ctx"),
        P(),
        P(("groups", "ctx"), None),
        P(("groups", "ctx"), None),
        P("groups"),
        P("ctx", None),
        P("ctx"),
        P(None, "ctx"),
    )
    out_specs = (P("groups", "ctx"), P("groups", "ctx"))
    return jax.shard_map(
        on_device, mesh=mesh, in_specs=in_specs, out_specs=out_specs, check_vma=False
    )
```

profile of v0, /device:TPU:0, one launch (start us, length us, event | category | flops | bytes accessed | tf_op | source)
XLA Modules:
  0.0 440.1 jit_solution(16993364083367760374)
XLA Ops:
  8.7 23.2 %all-gather = bf16[16,1,512]{2,1,0:T(2,128)(2,1)S(1)} all-gather(bf16[1,1,512]{2,1,0:T(2,128)(2,1)S(1)} %reshape.86), channel_id=1, replica_groups=mesh['groups'=2,'ctx'=16] {'ctx'}, dimensions={0}, use_global_device_ids=true | all-gather | bytes 17408 | tf_op jit(solution)/shard_map/all_gather | solution.py:21
  32.6 21.4 %all-gather.5.cloned.1.call-done = bf16[128,8192]{1,0:T(8,128)(2,1)} async-done(((bf16[128,512]{1,0:T(8,128)(2,1)}), bf16[128,8192]{1,0:T(8,128)(2,1)}) %all-gather.5.cloned.1.call-update) | async-done | bytes 2097168 | tf_op jit(solution)/shard_map/all_gather | solution.py:20
  62.0 243.6 %while.22 = (s32[]{:T(128)}, bf16[512,128]{1,0:T(8,128)(2,1)S(1)}, f32[512,128]{1,0:T(8,128)S(1)}, f32[512]{0:T(512)S(1)}, f32[512]{0:T(512)S(1)}, /*index=5*/s3...) while((s32[]{:T(128)}, bf16[512,128]{1,0:T(8,128)(2,1)S(1)}, ...), condition=%wide.region_5.6_spmd.clone, body=%wide.region_2.5_spmd.clone.sunk | while | flops 408687136 | bytes 17614000 | solution.py:101
  71.1 6.1 %collective-permute-done.3 = bf16[512]{0:T(512)(128)(2,1)S(1)} collective-permute-done((bf16[512]{0:T(512)(128)(2,1)S(1)}, bf16[512]{0:T(512)(128)(2,1)S(1)}, u32[]{:S(2)}, u32[]{:S(2)}) %collective-permute-start.3) | collective-permute-done | bytes 1056 | tf_op jit(solution)/shard_map/while/body/eval_jaxpr/ppermute | solution.py:15
  84.5 7.9 %collective-permute-done.3 = bf16[512]{0:T(512)(128)(2,1)S(1)} collective-permute-done((bf16[512]{0:T(512)(128)(2,1)S(1)}, bf16[512]{0:T(512)(128)(2,1)S(1)}, u32[]{:S(2)}, u32[]{:S(2)}) %collective-permute-start.3) | collective-permute-done | bytes 1056 | tf_op jit(solution)/shard_map/while/body/eval_jaxpr/ppermute | solution.py:15
  99.3 8.3 %collective-permute-done.3 = bf16[512]{0:T(512)(128)(2,1)S(1)} collective-permute-done((bf16[512]{0:T(512)(128)(2,1)S(1)}, bf16[512]{0:T(512)(128)(2,1)S(1)}, u32[]{:S(2)}, u32[]{:S(2)}) %collective-permute-start.3) | collective-permute-done | bytes 1056 | tf_op jit(solution)/shard_map/while/body/eval_jaxpr/ppermute | solution.py:15
  114.5 8.3 %collective-permute-done.3 = bf16[512]{0:T(512)(128)(2,1)S(1)} collective-permute-done((bf16[512]{0:T(512)(128)(2,1)S(1)}, bf16[512]{0:T(512)(128)(2,1)S(1)}, u32[]{:S(2)}, u32[]{:S(2)}) %collective-permute-start.3) | collective-permute-done | bytes 1056 | tf_op jit(solution)/shard_map/while/body/eval_jaxpr/ppermute | solution.py:15
  129.7 8.3 %collective-permute-done.3 = bf16[512]{0:T(512)(128)(2,1)S(1)} collective-permute-done((bf16[512]{0:T(512)(128)(2,1)S(1)}, bf16[512]{0:T(512)(128)(2,1)S(1)}, u32[]{:S(2)}, u32[]{:S(2)}) %collective-permute-start.3) | collective-permute-done | bytes 1056 | tf_op jit(solution)/shard_map/while/body/eval_jaxpr/ppermute | solution.py:15
  144.9 8.3 %collective-permute-done.3 = bf16[512]{0:T(512)(128)(2,1)S(1)} collective-permute-done((bf16[512]{0:T(512)(128)(2,1)S(1)}, bf16[512]{0:T(512)(128)(2,1)S(1)}, u32[]{:S(2)}, u32[]{:S(2)}) %collective-permute-start.3) | collective-permute-done | bytes 1056 | tf_op jit(solution)/shard_map/while/body/eval_jaxpr/ppermute | solution.py:15
  160.2 8.3 %collective-permute-done.3 = bf16[512]{0:T(512)(128)(2,1)S(1)} collective-permute-done((bf16[512]{0:T(512)(128)(2,1)S(1)}, bf16[512]{0:T(512)(128)(2,1)S(1)}, u32[]{:S(2)}, u32[]{:S(2)}) %collective-permute-start.3) | collective-permute-done | bytes 1056 | tf_op jit(solution)/shard_map/while/body/eval_jaxpr/ppermute | solution.py:15
  175.4 8.3 %collective-permute-done.3 = bf16[512]{0:T(512)(128)(2,1)S(1)} collective-permute-done((bf16[512]{0:T(512)(128)(2,1)S(1)}, bf16[512]{0:T(512)(128)(2,1)S(1)}, u32[]{:S(2)}, u32[]{:S(2)}) %collective-permute-start.3) | collective-permute-done | bytes 1056 | tf_op jit(solution)/shard_map/while/body/eval_jaxpr/ppermute | solution.py:15
  190.6 8.3 %collective-permute-done.3 = bf16[512]{0:T(512)(128)(2,1)S(1)} collective-permute-done((bf16[512]{0:T(512)(128)(2,1)S(1)}, bf16[512]{0:T(512)(128)(2,1)S(1)}, u32[]{:S(2)}, u32[]{:S(2)}) %collective-permute-start.3) | collective-permute-done | bytes 1056 | tf_op jit(solution)/shard_map/while/body/eval_jaxpr/ppermute | solution.py:15
  205.9 8.3 %collective-permute-done.3 = bf16[512]{0:T(512)(128)(2,1)S(1)} collective-permute-done((bf16[512]{0:T(512)(128)(2,1)S(1)}, bf16[512]{0:T(512)(128)(2,1)S(1)}, u32[]{:S(2)}, u32[]{:S(2)}) %collective-permute-start.3) | collective-permute-done | bytes 1056 | tf_op jit(solution)/shard_map/while/body/eval_jaxpr/ppermute | solution.py:15
  221.1 8.3 %collective-permute-done.3 = bf16[512]{0:T(512)(128)(2,1)S(1)} collective-permute-done((bf16[512]{0:T(512)(128)(2,1)S(1)}, bf16[512]{0:T(512)(128)(2,1)S(1)}, u32[]{:S(2)}, u32[]{:S(2)}) %collective-permute-start.3) | collective-permute-done | bytes 1056 | tf_op jit(solution)/shard_map/while/body/eval_jaxpr/ppermute | solution.py:15
  236.3 8.3 %collective-permute-done.3 = bf16[512]{0:T(512)(128)(2,1)S(1)} collective-permute-done((bf16[512]{0:T(512)(128)(2,1)S(1)}, bf16[512]{0:T(512)(128)(2,1)S(1)}, u32[]{:S(2)}, u32[]{:S(2)}) %collective-permute-start.3) | collective-permute-done | bytes 1056 | tf_op jit(solution)/shard_map/while/body/eval_jaxpr/ppermute | solution.py:15
  251.5 8.3 %collective-permute-done.3 = bf16[512]{0:T(512)(128)(2,1)S(1)} collective-permute-done((bf16[512]{0:T(512)(128)(2,1)S(1)}, bf16[512]{0:T(512)(128)(2,1)S(1)}, u32[]{:S(2)}, u32[]{:S(2)}) %collective-permute-start.3) | collective-permute-done | bytes 1056 | tf_op jit(solution)/shard_map/while/body/eval_jaxpr/ppermute | solution.py:15
  266.8 8.3 %collective-permute-done.3 = bf16[512]{0:T(512)(128)(2,1)S(1)} collective-permute-done((bf16[512]{0:T(512)(128)(2,1)S(1)}, bf16[512]{0:T(512)(128)(2,1)S(1)}, u32[]{:S(2)}, u32[]{:S(2)}) %collective-permute-start.3) | collective-permute-done | bytes 1056 | tf_op jit(solution)/shard_map/while/body/eval_jaxpr/ppermute | solution.py:15
  282.0 8.3 %collective-permute-done.3 = bf16[512]{0:T(512)(128)(2,1)S(1)} collective-permute-done((bf16[512]{0:T(512)(128)(2,1)S(1)}, bf16[512]{0:T(512)(128)(2,1)S(1)}, u32[]{:S(2)}, u32[]{:S(2)}) %collective-permute-start.3) | collective-permute-done | bytes 1056 | tf_op jit(solution)/shard_map/while/body/eval_jaxpr/ppermute | solution.py:15
  297.2 8.3 %collective-permute-done.3 = bf16[512]{0:T(512)(128)(2,1)S(1)} collective-permute-done((bf16[512]{0:T(512)(128)(2,1)S(1)}, bf16[512]{0:T(512)(128)(2,1)S(1)}, u32[]{:S(2)}, u32[]{:S(2)}) %collective-permute-start.3) | collective-permute-done | bytes 1056 | tf_op jit(solution)/shard_map/while/body/eval_jaxpr/ppermute | solution.py:15
  305.9 6.6 %convolution_bitcast_fusion = f32[8192,128]{0,1:T(8,128)} fusion(bf16[128,512]{1,0:T(8,128)(2,1)S(1)} %reshape.85, bf16[512,8192]{1,0:T(8,128)(2,1)} %param.19), kind=kOutput, calls=%fused_computation.22 | convolution fusion | flops 1073741824 | bytes 12713984 | tf_op jit(solution)/shard_map/dot_general | solution.py:104
  312.5 70.2 %reduce-scatter.2.cloned.1.call-done = f32[512,128]{0,1:T(8,128)} async-done(((f32[8192,128]{0,1:T(8,128)}), f32[512,128]{0,1:T(8,128)}) %reduce-scatter.2.cloned.1.call-update) | async-done | bytes 262160 | tf_op jit(solution)/shard_map/reduce_scatter | solution.py:103
  384.4 19.3 %all-gather.1 = bf16[16,1,512]{2,1,0:T(2,128)(2,1)S(1)} all-gather(bf16[1,1,512]{2,1,0:T(2,128)(2,1)S(1)} %reshape.88), channel_id=1, replica_groups=mesh['groups'=2,'ctx'=16] {'ctx'}, dimensions={0}, use_global_device_ids=true | all-gather | bytes 17408 | tf_op jit(solution)/shard_map/all_gather | solution.py:21
  403.7 21.7 %all-gather.7.cloned.1.call-done = bf16[128,8192]{1,0:T(8,128)(2,1)} async-done(((bf16[128,512]{1,0:T(8,128)(2,1)}), bf16[128,8192]{1,0:T(8,128)(2,1)}) %all-gather.7.cloned.1.call-update) | async-done | bytes 2097168 | tf_op jit(solution)/shard_map/all_gather | solution.py:20
  427.6 6.0 %fusion.35 = bf16[128,512]{1,0:T(8,128)(2,1)} fusion(bf16[8192,512]{1,0:T(8,128)(2,1)} %param.21, bf16[128,8192]{1,0:T(8,128)(2,1)} %all-gather.7.cloned.1.call-done, f32[8192]{0:T(1024)S(1)} %bitcast.20, f32[128]{0:T(128)S(1)} %add_rsqrt_fusion.1), kind=kOutput, calls=%fused_computation.39 | convolution fusion | flops 1078001664 | bytes 10650112 | tf_op jit(solution)/shard_map/dot_general | solution.py:26
  (355 shorter events, 124.4 us)
Async XLA Ops:
  7.2 46.8 %all-gather.5.cloned.1.call-start = ((), (), s32[]{:S(2)}) async-start(), calls=%async_computation.1 | async-start | bytes 2228224 | tf_op jit(solution)/shard_map/all_gather | solution.py:20
  7.9 374.8 %reduce-scatter.2.cloned.1.call-start = ((), (), s32[]{:S(2)}) async-start(), calls=%async_computation.2 | async-start | bytes 4456448 | tf_op jit(solution)/shard_map/reduce_scatter | solution.py:103
  68.5 8.6 %collective-permute-start.1 = (bf16[512,128]{1,0:T(8,128)(2,1)S(1)}, bf16[512,128]{1,0:T(8,128)(2,1)S(1)}, u32[]{:S(2)}, u32[]{:S(2)}) collective-permute-start(bf16[512,128]{1,0:T(8,128)(2,1)S(1)} %fusion.65), channel_id=1, source_target_pairs={{15,0},{0,1},{1,2},{2,3},{3,4},{4,5},{5,6},{6,7},{7,8},{8,9},{9,10... | collective-permute-start | bytes 393224 | tf_op jit(solution)/shard_map/while/body/eval_jaxpr/ppermute | solution.py:15
  83.8 8.6 %collective-permute-start.1 = (bf16[512,128]{1,0:T(8,128)(2,1)S(1)}, bf16[512,128]{1,0:T(8,128)(2,1)S(1)}, u32[]{:S(2)}, u32[]{:S(2)}) collective-permute-start(bf16[512,128]{1,0:T(8,128)(2,1)S(1)} %fusion.65), channel_id=1, source_target_pairs={{15,0},{0,1},{1,2},{2,3},{3,4},{4,5},{5,6},{6,7},{7,8},{8,9},{9,10... | collective-permute-start | bytes 393224 | tf_op jit(solution)/shard_map/while/body/eval_jaxpr/ppermute | solution.py:15
  99.0 8.6 %collective-permute-start.1 = (bf16[512,128]{1,0:T(8,128)(2,1)S(1)}, bf16[512,128]{1,0:T(8,128)(2,1)S(1)}, u32[]{:S(2)}, u32[]{:S(2)}) collective-permute-start(bf16[512,128]{1,0:T(8,128)(2,1)S(1)} %fusion.65), channel_id=1, source_target_pairs={{15,0},{0,1},{1,2},{2,3},{3,4},{4,5},{5,6},{6,7},{7,8},{8,9},{9,10... | collective-permute-start | bytes 393224 | tf_op jit(solution)/shard_map/while/body/eval_jaxpr/ppermute | solution.py:15
  99.1 8.6 %collective-permute-start = (bf16[512,128]{1,0:T(8,128)(2,1)S(1)}, bf16[512,128]{1,0:T(8,128)(2,1)S(1)}, u32[]{:S(2)}, u32[]{:S(2)}) collective-permute-start(bf16[512,128]{1,0:T(8,128)(2,1)S(1)} %copy.22), channel_id=1, source_target_pairs={{15,0},{0,1},{1,2},{2,3},{3,4},{4,5},{5,6},{6,7},{7,8},{8,9},{9,10... | collective-permute-start | bytes 393224 | tf_op jit(solution)/shard_map/while/body/eval_jaxpr/ppermute | solution.py:15
  114.2 8.6 %collective-permute-start.1 = (bf16[512,128]{1,0:T(8,128)(2,1)S(1)}, bf16[512,128]{1,0:T(8,128)(2,1)S(1)}, u32[]{:S(2)}, u32[]{:S(2)}) collective-permute-start(bf16[512,128]{1,0:T(8,128)(2,1)S(1)} %fusion.65), channel_id=1, source_target_pairs={{15,0},{0,1},{1,2},{2,3},{3,4},{4,5},{5,6},{6,7},{7,8},{8,9},{9,10... | collective-permute-start | bytes 393224 | tf_op jit(solution)/shard_map/while/body/eval_jaxpr/ppermute | solution.py:15
  114.3 8.6 %collective-permute-start = (bf16[512,128]{1,0:T(8,128)(2,1)S(1)}, bf16[512,128]{1,0:T(8,128)(2,1)S(1)}, u32[]{:S(2)}, u32[]{:S(2)}) collective-permute-start(bf16[512,128]{1,0:T(8,128)(2,1)S(1)} %copy.22), channel_id=1, source_target_pairs={{15,0},{0,1},{1,2},{2,3},{3,4},{4,5},{5,6},{6,7},{7,8},{8,9},{9,10... | collective-permute-start | bytes 393224 | tf_op jit(solution)/shard_map/while/body/eval_jaxpr/ppermute | solution.py:15
  129.5 8.6 %collective-permute-start.1 = (bf16[512,128]{1,0:T(8,128)(2,1)S(1)}, bf16[512,128]{1,0:T(8,128)(2,1)S(1)}, u32[]{:S(2)}, u32[]{:S(2)}) collective-permute-start(bf16[512,128]{1,0:T(8,128)(2,1)S(1)} %fusion.65), channel_id=1, source_target_pairs={{15,0},{0,1},{1,2},{2,3},{3,4},{4,5},{5,6},{6,7},{7,8},{8,9},{9,10... | collective-permute-start | bytes 393224 | tf_op jit(solution)/shard_map/while/body/eval_jaxpr/ppermute | solution.py:15
  144.7 8.6 %collective-permute-start.1 = (bf16[512,128]{1,0:T(8,128)(2,1)S(1)}, bf16[512,128]{1,0:T(8,128)(2,1)S(1)}, u32[]{:S(2)}, u32[]{:S(2)}) collective-permute-start(bf16[512,128]{1,0:T(8,128)(2,1)S(1)} %fusion.65), channel_id=1, source_target_pairs={{15,0},{0,1},{1,2},{2,3},{3,4},{4,5},{5,6},{6,7},{7,8},{8,9},{9,10... | collective-permute-start | bytes 393224 | tf_op jit(solution)/shard_map/while/body/eval_jaxpr/ppermute | solution.py:15
  144.7 8.6 %collective-permute-start = (bf16[512,128]{1,0:T(8,128)(2,1)S(1)}, bf16[512,128]{1,0:T(8,128)(2,1)S(1)}, u32[]{:S(2)}, u32[]{:S(2)}) collective-permute-start(bf16[512,128]{1,0:T(8,128)(2,1)S(1)} %copy.22), channel_id=1, source_target_pairs={{15,0},{0,1},{1,2},{2,3},{3,4},{4,5},{5,6},{6,7},{7,8},{8,9},{9,10... | collective-permute-start | bytes 393224 | tf_op jit(solution)/shard_map/while/body/eval_jaxpr/ppermute | solution.py:15
  159.9 8.6 %collective-permute-start.1 = (bf16[512,128]{1,0:T(8,128)(2,1)S(1)}, bf16[512,128]{1,0:T(8,128)(2,1)S(1)}, u32[]{:S(2)}, u32[]{:S(2)}) collective-permute-start(bf16[512,128]{1,0:T(8,128)(2,1)S(1)} %fusion.65), channel_id=1, source_target_pairs={{15,0},{0,1},{1,2},{2,3},{3,4},{4,5},{5,6},{6,7},{7,8},{8,9},{9,10... | collective-permute-start | bytes 393224 | tf_op jit(solution)/shard_map/while/body/eval_jaxpr/ppermute | solution.py:15
  160.0 8.6 %collective-permute-start = (bf16[512,128]{1,0:T(8,128)(2,1)S(1)}, bf16[512,128]{1,0:T(8,128)(2,1)S(1)}, u32[]{:S(2)}, u32[]{:S(2)}) collective-permute-start(bf16[512,128]{1,0:T(8,128)(2,1)S(1)} %copy.22), channel_id=1, source_target_pairs={{15,0},{0,1},{1,2},{2,3},{3,4},{4,5},{5,6},{6,7},{7,8},{8,9},{9,10... | collective-permute-start | bytes 393224 | tf_op jit(solution)/shard_map/while/body/eval_jaxpr/ppermute | solution.py:15
  175.1 8.6 %collective-permute-start.1 = (bf16[512,128]{1,0:T(8,128)(2,1)S(1)}, bf16[512,128]{1,0:T(8,128)(2,1)S(1)}, u32[]{:S(2)}, u32[]{:S(2)}) collective-permute-start(bf16[512,128]{1,0:T(8,128)(2,1)S(1)} %fusion.65), channel_id=1, source_target_pairs={{15,0},{0,1},{1,2},{2,3},{3,4},{4,5},{5,6},{6,7},{7,8},{8,9},{9,10... | collective-permute-start | bytes 393224 | tf_op jit(solution)/shard_map/while/body/eval_jaxpr/ppermute | solution.py:15
  175.2 8.6 %collective-permute-start = (bf16[512,128]{1,0:T(8,128)(2,1)S(1)}, bf16[512,128]{1,0:T(8,128)(2,1)S(1)}, u32[]{:S(2)}, u32[]{:S(2)}) collective-permute-start(bf16[512,128]{1,0:T(8,128)(2,1)S(1)} %copy.22), channel_id=1, source_target_pairs={{15,0},{0,1},{1,2},{2,3},{3,4},{4,5},{5,6},{6,7},{7,8},{8,9},{9,10... | collective-permute-start | bytes 393224 | tf_op jit(solution)/shard_map/while/body/eval_jaxpr/ppermute | solution.py:15
  190.4 8.6 %collective-permute-start.1 = (bf16[512,128]{1,0:T(8,128)(2,1)S(1)}, bf16[512,128]{1,0:T(8,128)(2,1)S(1)}, u32[]{:S(2)}, u32[]{:S(2)}) collective-permute-start(bf16[512,128]{1,0:T(8,128)(2,1)S(1)} %fusion.65), channel_id=1, source_target_pairs={{15,0},{0,1},{1,2},{2,3},{3,4},{4,5},{5,6},{6,7},{7,8},{8,9},{9,10... | collective-permute-start | bytes 393224 | tf_op jit(solution)/shard_map/while/body/eval_jaxpr/ppermute | solution.py:15
  205.6 8.6 %collective-permute-start.1 = (bf16[512,128]{1,0:T(8,128)(2,1)S(1)}, bf16[512,128]{1,0:T(8,128)(2,1)S(1)}, u32[]{:S(2)}, u32[]{:S(2)}) collective-permute-start(bf16[512,128]{1,0:T(8,128)(2,1)S(1)} %fusion.65), channel_id=1, source_target_pairs={{15,0},{0,1},{1,2},{2,3},{3,4},{4,5},{5,6},{6,7},{7,8},{8,9},{9,10... | collective-permute-start | bytes 393224 | tf_op jit(solution)/shard_map/while/body/eval_jaxpr/ppermute | solution.py:15
  220.8 8.6 %collective-permute-start.1 = (bf16[512,128]{1,0:T(8,128)(2,1)S(1)}, bf16[512,128]{1,0:T(8,128)(2,1)S(1)}, u32[]{:S(2)}, u32[]{:S(2)}) collective-permute-start(bf16[512,128]{1,0:T(8,128)(2,1)S(1)} %fusion.65), channel_id=1, source_target_pairs={{15,0},{0,1},{1,2},{2,3},{3,4},{4,5},{5,6},{6,7},{7,8},{8,9},{9,10... | collective-permute-start | bytes 393224 | tf_op jit(solution)/shard_map/while/body/eval_jaxpr/ppermute | solution.py:15
  236.0 8.6 %collective-permute-start.1 = (bf16[512,128]{1,0:T(8,128)(2,1)S(1)}, bf16[512,128]{1,0:T(8,128)(2,1)S(1)}, u32[]{:S(2)}, u32[]{:S(2)}) collective-permute-start(bf16[512,128]{1,0:T(8,128)(2,1)S(1)} %fusion.65), channel_id=1, source_target_pairs={{15,0},{0,1},{1,2},{2,3},{3,4},{4,5},{5,6},{6,7},{7,8},{8,9},{9,10... | collective-permute-start | bytes 393224 | tf_op jit(solution)/shard_map/while/body/eval_jaxpr/ppermute | solution.py:15
  251.3 8.6 %collective-permute-start.1 = (bf16[512,128]{1,0:T(8,128)(2,1)S(1)}, bf16[512,128]{1,0:T(8,128)(2,1)S(1)}, u32[]{:S(2)}, u32[]{:S(2)}) collective-permute-start(bf16[512,128]{1,0:T(8,128)(2,1)S(1)} %fusion.65), channel_id=1, source_target_pairs={{15,0},{0,1},{1,2},{2,3},{3,4},{4,5},{5,6},{6,7},{7,8},{8,9},{9,10... | collective-permute-start | bytes 393224 | tf_op jit(solution)/shard_map/while/body/eval_jaxpr/ppermute | solution.py:15
  266.5 8.6 %collective-permute-start.1 = (bf16[512,128]{1,0:T(8,128)(2,1)S(1)}, bf16[512,128]{1,0:T(8,128)(2,1)S(1)}, u32[]{:S(2)}, u32[]{:S(2)}) collective-permute-start(bf16[512,128]{1,0:T(8,128)(2,1)S(1)} %fusion.65), channel_id=1, source_target_pairs={{15,0},{0,1},{1,2},{2,3},{3,4},{4,5},{5,6},{6,7},{7,8},{8,9},{9,10... | collective-permute-start | bytes 393224 | tf_op jit(solution)/shard_map/while/body/eval_jaxpr/ppermute | solution.py:15
  281.7 8.6 %collective-permute-start.1 = (bf16[512,128]{1,0:T(8,128)(2,1)S(1)}, bf16[512,128]{1,0:T(8,128)(2,1)S(1)}, u32[]{:S(2)}, u32[]{:S(2)}) collective-permute-start(bf16[512,128]{1,0:T(8,128)(2,1)S(1)} %fusion.65), channel_id=1, source_target_pairs={{15,0},{0,1},{1,2},{2,3},{3,4},{4,5},{5,6},{6,7},{7,8},{8,9},{9,10... | collective-permute-start | bytes 393224 | tf_op jit(solution)/shard_map/while/body/eval_jaxpr/ppermute | solution.py:15
  296.9 8.6 %collective-permute-start.1 = (bf16[512,128]{1,0:T(8,128)(2,1)S(1)}, bf16[512,128]{1,0:T(8,128)(2,1)S(1)}, u32[]{:S(2)}, u32[]{:S(2)}) collective-permute-start(bf16[512,128]{1,0:T(8,128)(2,1)S(1)} %fusion.65), channel_id=1, source_target_pairs={{15,0},{0,1},{1,2},{2,3},{3,4},{4,5},{5,6},{6,7},{7,8},{8,9},{9,10... | collective-permute-start | bytes 393224 | tf_op jit(solution)/shard_map/while/body/eval_jaxpr/ppermute | solution.py:15
  312.5 113.0 %all-gather.7.cloned.1.call-start = ((), (), s32[]{:S(2)}) async-start(), calls=%async_computation.3 | async-start | bytes 2228224 | tf_op jit(solution)/shard_map/all_gather | solution.py:20
  (46 other events, 510.1 us)
Sparse Core Ops, SparseCore 0:
  10.1 43.7 all-gather.4
  312.6 70.0 reduce-scatter.1
  385.5 39.9 all-gather.6
where the time goes:
time: 442 us; the launch traced here: 440 us
  waiting for transfers between devices  245 us (55%)
  matrix products  71.6 us (16%)
  blocking collectives  42.5 us (10%)
  local copies, waits for them, and re-layouts  39.4 us (9%)
  other arithmetic  18.6 us (4%)
  between operations  13.9 us (3%)
  starting transfers between devices  6.57 us (1%)
    ppermute x64, waiting for transfers between devices, shifted(): return lax.ppermute(block, axis, route)  131 us
    reduce_scatter x1, waiting for transfers between devices, on_device(): lax.psum_scatter(lax.dot_general(out_weight, attended, (((0,), (1,)), (()...  70.2 us
    all_gather x2, waiting for transfers between devices, normalize_project(): lax.all_gather(share, 'ctx', axis=1, tiled=True)  43.1 us
    all_gather x2, blocking collectives, normalize_project(): lax.all_gather(gain_share, 'ctx', axis=0, tiled=True)  42.5 us
    broadcast_in_dim x48, local copies, waits for them, and re-layouts, masked_scores(): scores = jnp.where(allowed[:, None, :], scores, -jnp.inf)  38.2 us
    dot_general x16, matrix products, visit(): jnp.dot(expo.astype(jnp.bfloat16), values, preferred_element_type=jnp.flo...  26.9 us
    dot_general x16, matrix products, masked_scores(): lax.dot_general(query_rows, keys, (((1,), (1,)), ((), ())), preferred_ele...  26.8 us
    dot_general x2, matrix products, normalize_project(): return jnp.dot(normed, weight, preferred_element_type=jnp.float32)  11.3 us
  transfers between devices with their start and end apart: 67, of which 19 were waited for; matrix products, arithmetic and copies ran while one was open for 0% of the time, Pallas kernels for 0%

commit v1 on v0

v1 whole, which is shorter than its diff:
```python
import jax
import jax.numpy as jnp
from jax import lax
from jax.sharding import PartitionSpec as P

BLK = 128


EPSILON = 1e-05


def normalize_project(share, gain_share, weight):
    whole, gains = (
        lax.all_gather(share, "ctx", axis=1, tiled=True),
        lax.all_gather(gain_share, "ctx", axis=0, tiled=True),
    )
    values = whole.astype(jnp.float32)
    factor = lax.rsqrt(jnp.mean(values * values, axis=1, keepdims=True) + EPSILON)
    normed = (values * factor * gains.astype(jnp.float32)).astype(jnp.bfloat16)
    return jnp.dot(normed, weight, preferred_element_type=jnp.float32)


def on_device(
    hidden,
    attn_gain,
    q_weight,
    q_gain,
    key_cache,
    value_cache,
    block_limit,
    out_weight,
    next_gain,
    next_weight,
):
    queries = hidden.shape[0]
    head_dim = q_gain.shape[0]
    devices = lax.axis_size("ctx")
    query = normalize_project(hidden, attn_gain, q_weight)
    heads_here = query.shape[1] // head_dim
    heads_total = heads_here * devices
    kv_heads = key_cache.shape[1] // head_dim
    group_size = heads_total // kv_heads
    shaped = query.reshape(queries, heads_here, head_dim)
    head_mean = jnp.mean(shaped * shaped, axis=-1, keepdims=True)
    query_normed = (shaped * lax.rsqrt(head_mean + EPSILON) * q_gain.astype(jnp.float32)).astype(
        jnp.bfloat16
    )
    local_tokens = key_cache.shape[0]
    device = lax.axis_index("ctx")
    blocks_here = (device * local_tokens + jnp.arange(local_tokens, dtype=jnp.int32)) // BLK
    allowed = blocks_here[None, :] <= block_limit[:, None]
    scale = head_dim ** (-0.5)
    stacked = jnp.swapaxes(query_normed, 0, 1)
    gathered = lax.all_gather(stacked, "ctx", axis=0, tiled=True)
    gathered = gathered.reshape(kv_heads, group_size * queries, head_dim)
    mask = jnp.tile(allowed, (group_size, 1))

    def one_group(group):
        keys = lax.dynamic_slice_in_dim(key_cache, group * head_dim, head_dim, 1)
        values = lax.dynamic_slice_in_dim(value_cache, group * head_dim, head_dim, 1)
        rows = lax.dynamic_index_in_dim(gathered, group, 0, keepdims=False)
        scores = lax.dot_general(
            rows, keys, (((1,), (1,)), ((), ())), preferred_element_type=jnp.float32
        )
        scores = jnp.where(mask, scores * scale, -jnp.inf)
        top = jnp.maximum(jnp.max(scores, axis=1), -1e30)
        expo = jnp.exp(scores - top[:, None])
        sums = jnp.dot(expo.astype(jnp.bfloat16), values, preferred_element_type=jnp.float32)
        return sums, top, jnp.sum(expo, axis=1)

    sums, top, total = lax.map(one_group, jnp.arange(kv_heads, dtype=jnp.int32))
    decay = jnp.exp(top - lax.pmax(top, "ctx"))
    sums = (sums * decay[:, :, None]).astype(jnp.bfloat16).reshape(heads_total, queries, head_dim)
    total = (total * decay).reshape(heads_total, queries)
    sums = lax.psum_scatter(sums, "ctx", scatter_dimension=0, tiled=True)
    total = lax.psum_scatter(total, "ctx", scatter_dimension=0, tiled=True)
    attended = (sums.astype(jnp.float32) / total[:, :, None]).astype(jnp.bfloat16)
    attended = jnp.swapaxes(attended, 0, 1).reshape(queries, heads_here * head_dim)
    mixed = lax.psum_scatter(
        lax.dot_general(
            out_weight, attended, (((0,), (1,)), ((), ())), preferred_element_type=jnp.float32
        ),
        "ctx",
        scatter_dimension=0,
        tiled=True,
    )
    new_hidden = (hidden.astype(jnp.float32) + mixed.T).astype(jnp.bfloat16)
    next_queries = normalize_project(new_hidden, next_gain, next_weight).astype(jnp.bfloat16)
    return (new_hidden, next_queries)


def solution(mesh):
    in_specs = (
        P("groups", "ctx"),
        P("ctx"),
        P(None, "ctx"),
        P(),
        P(("groups", "ctx"), None),
        P(("groups", "ctx"), None),
        P("groups"),
        P("ctx", None),
        P("ctx"),
        P(None, "ctx"),
    )
    out_specs = (P("groups", "ctx"), P("groups", "ctx"))
    return jax.shard_map(
        on_device, mesh=mesh, in_specs=in_specs, out_specs=out_specs, check_vma=False
    )
```

time: 442 us -> 451 us (1.020)
  blocking collectives: 42.5 us -> 160 us
  waiting for transfers between devices: 245 us -> 156 us
  local copies, waits for them, and re-layouts: 39.4 us -> 7.7 us
  loops' own time: 2.77 us -> 21.1 us
  other arithmetic: 18.6 us -> 32 us
  matrix products: 71.6 us -> 58.6 us
  starting transfers between devices: 6.57 us -> 0.2 us
    ppermute x64 -> x0, waiting for transfers between devices: 131 us -> none  [shifted(): return lax.ppermute(block, axis, route)]
    pmax x0 -> x1, blocking collectives: none -> 59.4 us  [on_device(): decay = jnp.exp(top - lax.pmax(top, 'ctx'))]
    unnamed x0 -> x1, blocking collectives: none -> 57.8 us
    all_gather x0 -> x1, waiting for transfers between devices: none -> 40.4 us  [on_device(): gathered = lax.all_gather(stacked, 'ctx', axis=0, tiled=True)]
    broadcast_in_dim x48 -> x0, local copies, waits for them, and re-layouts: 38.2 us -> none  [masked_scores(): scores = jnp.where(allowed[:, None, :], scores, -jnp.inf)]
    another operation x1, loops' own time: 2.77 us -> 21.1 us  [on_device(): sums, top, total = lax.map(one_group, jnp.arange(kv_heads, dtype=jnp.int32))]
    dot_general x32 -> x16, matrix products: 53.7 us -> 40.7 us  [the longest x8 22.3 us: one_group(): jnp.dot(expo.astype(jnp.bfloat16), values, preferred_element_type=jnp.flo...]
    reduce_sum x16 -> x8, other arithmetic: 7.96 us -> 19.3 us  [one_group(): return (sums, top, jnp.sum(expo, axis=1))]
  transfers between devices with their start and end apart: 67 -> 5, of which waited for: 19 -> 5; matrix products, arithmetic and copies ran while one was open for 0% -> 0% of each run, Pallas kernels for 0% -> 0%
where the time goes in v1:
time: 451 us; the launch traced here: 450 us
  blocking collectives  160 us (35%)
  waiting for transfers between devices  156 us (35%)
  matrix products  58.6 us (13%)
  other arithmetic  32 us (7%)
  loops' own time  21.1 us (5%)
  between operations  14.6 us (3%)
  local copies, waits for them, and re-layouts  7.7 us (2%)
    reduce_scatter x1, waiting for transfers between devices, on_device(): lax.psum_scatter(lax.dot_general(out_weight, attended, (((0,), (1,)), (()...  71.8 us
    pmax x1, blocking collectives, on_device(): decay = jnp.exp(top - lax.pmax(top, 'ctx'))  59.4 us
    unnamed x1, blocking collectives  57.8 us
    all_gather x2, waiting for transfers between devices, normalize_project(): lax.all_gather(share, 'ctx', axis=1, tiled=True)  43.1 us
    all_gather x2, blocking collectives, normalize_project(): lax.all_gather(gain_share, 'ctx', axis=0, tiled=True)  42.5 us
    all_gather x1, waiting for transfers between devices, on_device(): gathered = lax.all_gather(stacked, 'ctx', axis=0, tiled=True)  40.4 us
    dot_general x8, matrix products, one_group(): jnp.dot(expo.astype(jnp.bfloat16), values, preferred_element_type=jnp.flo...  22.3 us
    another operation x1, loops' own time, on_device(): sums, top, total = lax.map(one_group, jnp.arange(kv_heads, dtype=jnp.int32))  21.1 us
  transfers between devices with their start and end apart: 5, of which 5 were waited for; matrix products, arithmetic and copies ran while one was open for 0% of the time, Pallas kernels for 0%

profile of v1, /device:TPU:0, one launch (start us, length us, event | category | flops | bytes accessed | tf_op | source)
XLA Modules:
  0.0 450.3 jit_solution(18239864491225797498)
XLA Ops:
  8.6 23.2 %all-gather = bf16[16,1,512]{2,1,0:T(2,128)(2,1)S(1)} all-gather(bf16[1,1,512]{2,1,0:T(2,128)(2,1)S(1)} %reshape.113), channel_id=1, replica_groups=mesh['groups'=2,'ctx'=16] {'ctx'}, dimensions={0}, use_global_device_ids=true | all-gather | bytes 17408 | tf_op jit(solution)/shard_map/all_gather | solution.py:15
  32.5 21.4 %all-gather.6.cloned.1.call-done = bf16[128,8192]{1,0:T(8,128)(2,1)} async-done(((bf16[128,512]{1,0:T(8,128)(2,1)}), bf16[128,8192]{1,0:T(8,128)(2,1)}) %all-gather.6.cloned.1.call-update) | async-done | bytes 2097168 | tf_op jit(solution)/shard_map/all_gather | solution.py:14
  56.0 5.3 %fusion.21 = f32[128,512]{1,0:T(8,128)S(1)} fusion(bf16[8192,512]{1,0:T(8,128)(2,1)} %param.14, bf16[128,8192]{1,0:T(8,128)(2,1)} %all-gather.6.cloned.1.call-done, f32[8192]{0:T(1024)S(1)} %bitcast.75, f32[128]{0:T(128)S(1)} %add_rsqrt_fusion.2), kind=kOutput, calls=%fused_computation.29 | convolution fusion | flops 1077936128 | bytes 10781184 | tf_op jit(solution)/shard_map/dot_general | solution.py:20
  62.9 40.4 %all-gather.8.cloned.1.call-done = bf16[64,128,128]{2,1,0:T(8,128)(2,1)} async-done(((bf16[4,128,128]{2,1,0:T(8,128)(2,1)}), bf16[64,128,128]{2,1,0:T(8,128)(2,1)}) %all-gather.8.cloned.1.call-update) | async-done | bytes 2097168 | tf_op jit(solution)/shard_map/all_gather | solution.py:54
  103.3 87.2 %while.15 = (s32[]{:T(128)}, f32[8,1024,128]{2,1,0:T(8,128)}, f32[8,1024]{1,0:T(8,128)S(1)}, f32[8,1024]{1,0:T(8,128)S(1)}, s32[8]{0:T(128)S(1)}, /*index=5*/bf1...) while((s32[]{:T(128)}, f32[8,1024,128]{2,1,0:T(8,128)}, ...), condition=%wide.region_5.6_spmd.clone, body=%wide.region_2.5_spmd.clone.sunk | while | flops 817888256 | bytes 20878068 | solution.py:71
  108.8 2.4 fusion.53
  111.2 2.8 fusion.54
  119.7 2.4 fusion.53
  122.1 2.8 fusion.54
  130.6 2.4 fusion.53
  133.0 2.8 fusion.54
  143.9 2.8 fusion.54
  154.8 2.8 fusion.54
  165.7 2.8 fusion.54
  176.6 2.8 fusion.54
  187.5 2.8 fusion.54
  190.5 59.4 %pmax.7 = f32[8,1024]{1,0:T(8,128)S(1)} all-reduce(f32[8,1024]{1,0:T(8,128)S(1)} %get-tuple-element.52), channel_id=1, replica_groups=mesh['groups'=2,'ctx'=16] {'ctx'}, use_global_device_ids=true, to_apply=%region_6.7 | all-reduce | flops 8192 | bytes 65536 | tf_op jit(solution)/shard_map/pmax | solution.py:72
  249.9 3.9 multiply_convert_fusion
  255.1 57.8 %all-reduce = f32[64,128]{1,0:T(8,128)S(1)} all-reduce(f32[64,128]{1,0:T(8,128)S(1)} %reshape.111), channel_id=3, replica_groups=mesh['groups'=2,'ctx'=16] {'ctx'}, use_global_device_ids=true, to_apply=%region_8.9.clone | all-reduce | flops 8192 | bytes 65536
  314.5 6.6 %convolution_bitcast_fusion.1 = f32[8192,128]{0,1:T(8,128)} fusion(bf16[128,512]{0,1:T(8,128)(2,1)S(1)} %bitcast.73, bf16[512,8192]{1,0:T(8,128)(2,1)} %param.19), kind=kOutput, calls=%fused_computation.16 | convolution fusion | flops 1073741824 | bytes 12713984 | tf_op jit(solution)/shard_map/dot_general | solution.py:80
  321.2 71.8 %reduce-scatter.5.cloned.1.call-done = f32[512,128]{0,1:T(8,128)} async-done(((f32[8192,128]{0,1:T(8,128)}), f32[512,128]{0,1:T(8,128)}) %reduce-scatter.5.cloned.1.call-update) | async-done | bytes 262160 | tf_op jit(solution)/shard_map/reduce_scatter | solution.py:79
  394.6 19.3 %all-gather.1 = bf16[16,1,512]{2,1,0:T(2,128)(2,1)S(1)} all-gather(bf16[1,1,512]{2,1,0:T(2,128)(2,1)S(1)} %reshape.115), channel_id=1, replica_groups=mesh['groups'=2,'ctx'=16] {'ctx'}, dimensions={0}, use_global_device_ids=true | all-gather | bytes 17408 | tf_op jit(solution)/shard_map/all_gather | solution.py:15
  414.0 21.7 %all-gather.10.cloned.1.call-done = bf16[128,8192]{1,0:T(8,128)(2,1)} async-done(((bf16[128,512]{1,0:T(8,128)(2,1)}), bf16[128,8192]{1,0:T(8,128)(2,1)}) %all-gather.10.cloned.1.call-update) | async-done | bytes 2097168 | tf_op jit(solution)/shard_map/all_gather | solution.py:14
  437.8 6.0 %fusion.27 = bf16[128,512]{1,0:T(8,128)(2,1)} fusion(bf16[8192,512]{1,0:T(8,128)(2,1)} %param.21, bf16[128,8192]{1,0:T(8,128)(2,1)} %all-gather.10.cloned.1.call-done, f32[8192]{0:T(1024)S(1)} %bitcast.76, f32[128]{0:T(128)S(1)} %add_rsqrt_fusion.1), kind=kOutput, calls=%fused_computation.34 | convolution fusion | flops 1078001664 | bytes 10650112 | tf_op jit(solution)/shard_map/dot_general | solution.py:20
  (91 shorter events, 48.2 us)
Async XLA Ops:
  7.2 46.8 %all-gather.6.cloned.1.call-start = ((), (), s32[]{:S(2)}) async-start(), calls=%async_computation.2 | async-start | bytes 2228224 | tf_op jit(solution)/shard_map/all_gather | solution.py:14
  7.9 95.4 %all-gather.8.cloned.1.call-start = ((), (), s32[]{:S(2)}) async-start(), calls=%async_computation.3 | async-start | bytes 2228224 | tf_op jit(solution)/shard_map/all_gather | solution.py:54
  56.0 6.7 %copy-start.2 = (s32[128]{0:T(128)S(1)}, s32[128]{0:T(128)}, u32[]{:S(2)}) copy-start(s32[128]{0:T(128)} %param.18) | copy-start | bytes 1540
  62.6 250.7 %reduce-scatter.3.cloned.1.call-start = ((), (), s32[]{:S(2)}) async-start(), calls=%async_computation.4 | async-start | bytes 2228224 | tf_op jit(solution)/shard_map/reduce_scatter | solution.py:75
  249.9 4.0 copy-start.3
  253.8 139.1 %reduce-scatter.5.cloned.1.call-start = ((), (), s32[]{:S(2)}) async-start(), calls=%async_computation.5 | async-start | bytes 4456448 | tf_op jit(solution)/shard_map/reduce_scatter | solution.py:79
  321.1 71.9 %copy-start = (bf16[128,512]{1,0:T(8,128)(2,1)S(1)}, bf16[128,512]{1,0:T(8,128)(2,1)}, u32[]{:S(2)}) copy-start(bf16[128,512]{1,0:T(8,128)(2,1)} %param.12) | copy-start | bytes 393220
  321.1 73.5 %copy-start.1 = (bf16[512]{0:T(512)(128)(2,1)S(1)}, bf16[512]{0:T(512)(128)(2,1)}, u32[]{:S(2)}) copy-start(bf16[512]{0:T(512)(128)(2,1)} %param.20) | copy-start | bytes 3076
  321.1 114.6 %all-gather.10.cloned.1.call-start = ((), (), s32[]{:S(2)}) async-start(), calls=%async_computation.6 | async-start | bytes 2228224 | tf_op jit(solution)/shard_map/all_gather | solution.py:14
Sparse Core Ops, SparseCore 0:
  10.1 43.7 all-gather.5
  62.7 40.5 all-gather.7
  253.9 59.2 reduce-scatter.2
  321.3 71.6 reduce-scatter.4
  395.5 40.1 all-gather.9

commit v2 on v1

v2 whole, which is shorter than its diff:
```python
import functools
import math

import jax
import jax.numpy as jnp
from jax import lax
from jax.experimental import pallas as pl
from jax.experimental.pallas import tpu as pltpu
from jax.sharding import PartitionSpec as P

BLK = 128
EPSILON = 1e-05
MESH = pl.DeviceIdType.MESH
BF16, F32 = jnp.bfloat16, jnp.float32


def loop(count, body):
    def step(i, carry):
        body(i)
        return carry

    lax.fori_loop(0, count, step, 0)


def kernel(
    n,
    group_size,
    block_in,
    q_gain_ref,
    limit_ref,
    qw_hbm,
    key_hbm,
    value_hbm,
    ow_hbm,
    nw_hbm,
    hidden_out,
    next_out,
    qw,
    keys,
    values,
    ow,
    nw,
    first,
    queries_all,
    second,
    sums,
    stats,
    mixed,
    sums_core,
    stats_core,
    mixed_core,
    sums_y,
    stats_y,
    mixed_y,
    sums_up,
    stats_up,
    mixed_up,
    sums_down,
    stats_down,
    mixed_down,
    acc,
    squares,
    limits,
    attended,
    sems,
    local_sems,
):
    depth = n // 4
    me = lax.axis_index("ctx")
    core, y, z = lax.rem(me, 2), lax.rem(me // 2, 2), me // 4
    rows, width = hidden_out.shape
    features = n * width
    head_dim = q_gain_ref.shape[1]
    heads = width // head_dim
    tokens = keys.shape[0]

    def at(zz, yy, cc):
        return zz * 4 + yy * 2 + cc

    other_core, other_y = at(z, y, 1 - core), at(z, 1 - y, core)
    above, below = at(z + 1, y, core), at(z - 1, y, core)

    loads = [
        pltpu.make_async_copy(src, dst, local_sems.at[i])
        for i, (src, dst) in enumerate(
            [
                (block_in, first.at[me]),
                (qw_hbm, qw),
                (key_hbm, keys),
                (value_hbm, values),
                (ow_hbm, ow),
                (nw_hbm, nw),
            ]
        )
    ]
    for load in loads:
        load.start()

    barrier = pltpu.get_barrier_semaphore()

    def greet(device):
        pl.semaphore_signal(barrier, inc=1, device_id={"ctx": device}, device_id_type=MESH)

    greet(other_core)
    greet(other_y)
    pl.when(z + 1 < depth)(lambda: greet(above))
    pl.when(z > 0)(lambda: greet(below))
    peers = 2 + jnp.where(z + 1 < depth, 1, 0) + jnp.where(z > 0, 1, 0)
    pl.semaphore_wait(barrier, peers)

    for head in range(heads):
        limits[head * rows : (head + 1) * rows, :] = jnp.broadcast_to(limit_ref[...], (rows, BLK))

    def remote(src, dst, send, recv, device):
        return pltpu.make_async_remote_copy(
            src_ref=src,
            dst_ref=dst,
            send_sem=sems.at[send],
            recv_sem=sems.at[recv],
            device_id={"ctx": device},
            device_id_type=MESH,
        )

    used = [0]
    drains = []

    def gather(buffer):
        base = used[0]
        used[0] += n + 5 * depth
        send = base + n

        def copy(block, device, sem):
            return remote(buffer.at[block], buffer.at[block], sem, base + block, device)

        def to_above(zz):
            return copy(at(zz, y, core), above, send + zz)

        def to_below(zz):
            return copy(at(zz, y, core), below, send + depth + zz)

        def to_y(zz):
            return copy(at(zz, y, core), other_y, send + 2 * depth + zz)

        def to_core(zz, yy):
            return copy(at(zz, yy, core), other_core, send + 3 * depth + 2 * zz + yy)

        def arrive(block):
            copy(block, other_core, send).wait_recv()

        def column(step, sign):
            zz = z + sign * step

            @pl.when((zz >= 0) & (zz < depth))
            def _():
                if step > 0:
                    arrive(at(zz, y, core))
                if step == 0 or sign < 0:
                    pl.when(z + 1 < depth)(lambda: to_above(zz).start())
                if step == 0 or sign > 0:
                    pl.when(z > 0)(lambda: to_below(zz).start())
                to_y(zz).start()
                to_core(zz, y).start()

        def beside(step, sign):
            zz = z + sign * step

            @pl.when((zz >= 0) & (zz < depth))
            def _():
                arrive(at(zz, 1 - y, core))
                to_core(zz, 1 - y).start()

        for step in range(depth + 1):
            if step < depth:
                for sign in (-1, 1) if step else (-1,):
                    column(step, sign)
            if step > 0:
                for sign in (-1, 1) if step > 1 else (-1,):
                    beside(step - 1, sign)

        def drain():
            def one(zz):
                pl.when((zz <= z) & (z + 1 < depth))(lambda: to_above(zz).wait_send())
                pl.when((zz >= z) & (z > 0))(lambda: to_below(zz).wait_send())
                to_y(zz).wait_send()
                to_core(zz, 0).wait_send()
                to_core(zz, 1).wait_send()

            loop(depth, one)

        drains.append(drain)
        return arrive

    def reduce(arrays, compute, combine):
        starts = []
        for _ in arrays:
            starts.append(used[0])
            used[0] += 10 * depth

        def copies(kind, zz, yy=0):
            made = []
            for base, (part, from_core, from_y, from_below, from_above) in zip(starts, arrays):
                if kind == 0:
                    slot, room, where = 2 * zz + yy, 2 * depth, 0
                    src, dst, device = part.at[at(zz, yy, 1 - core)], from_core, other_core
                elif kind == 1:
                    slot, room, where = zz, depth, 4 * depth
                    src, dst, device = part.at[at(zz, 1 - y, core)], from_y, other_y
                elif kind == 2:
                    slot, room, where = zz, depth, 6 * depth
                    src, dst, device = part.at[at(zz, y, core)], from_below, above
                else:
                    slot, room, where = zz, depth, 8 * depth
                    src, dst, device = part.at[at(zz, y, core)], from_above, below
                sem = base + where + slot
                made.append(remote(src, dst.at[slot], sem, sem + room, device))
            return made

        def begin(*which):
            for copy in copies(*which):
                copy.start()

        def received(*which):
            for copy in copies(*which):
                copy.wait_recv()

        def sent(*which):
            for copy in copies(*which):
                copy.wait_send()

        def add(block, which, slot):
            combine(block, [array[which].at[slot] for array in arrays])

        def send_core(i):
            zz, yy = lax.rem(i, depth), jnp.where(i < depth, 1 - y, y)
            compute(at(zz, yy, 1 - core))
            begin(0, zz, yy)

        def send_y(zz):
            block = at(zz, 1 - y, core)
            compute(block)
            received(0, zz, 1 - y)
            add(block, 1, 2 * zz + 1 - y)
            begin(1, zz)

        def keep(zz):
            block = at(zz, y, core)
            compute(block)
            received(0, zz, y)
            add(block, 1, 2 * zz + y)
            received(1, zz)
            add(block, 2, zz)

        loop(2 * depth, send_core)
        loop(depth, send_y)
        loop(depth, keep)

        def along(k):
            high, low = depth - 1 - k, k

            @pl.when(high > z)
            def _():
                @pl.when(z > 0)
                def _():
                    received(2, high)
                    add(at(high, y, core), 3, high)

                begin(2, high)

            @pl.when(low < z)
            def _():
                @pl.when(z + 1 < depth)
                def _():
                    received(3, low)
                    add(at(low, y, core), 4, low)

                begin(3, low)

        loop(depth, along)

        @pl.when(z > 0)
        def _():
            received(2, z)
            add(me, 3, z)

        @pl.when(z + 1 < depth)
        def _():
            received(3, z)
            add(me, 4, z)

        def drain():
            def one(zz):
                sent(0, zz, 0)
                sent(0, zz, 1)
                sent(1, zz)
                pl.when(zz > z)(lambda: sent(2, zz))
                pl.when(zz < z)(lambda: sent(3, zz))

            loop(depth, one)

        drains.append(drain)

    def project(buffer, gain_row, weight, arrive):
        acc[...] = jnp.zeros_like(acc)
        squares[...] = jnp.zeros_like(squares)

        def term(block):
            part = buffer[block, :rows, :].astype(F32)
            gain = first[block, rows : rows + 16, :].astype(F32)[gain_row : gain_row + 1, :]
            squared = part * part
            total = squared[:, :BLK]
            for start in range(BLK, width, BLK):
                total += squared[:, start : start + BLK]
            squares[...] += total
            depth_rows = pl.ds(pl.multiple_of(block * width, width), width)
            acc[...] += jnp.dot(
                (part * gain).astype(BF16), weight[depth_rows, :], preferred_element_type=F32
            )

        loop(n // 2, lambda i: term(2 * i + core))

        def last(i):
            block = 2 * i + 1 - core
            arrive(block)
            term(block)

        loop(n // 2, last)
        mean = jnp.sum(squares[...], axis=1, keepdims=True) * (1.0 / features)
        return acc[...] * lax.rsqrt(mean + EPSILON)

    loads[0].wait()
    arrive = gather(first)
    loads[1].wait()
    query = project(first, 0, qw, arrive)
    for head in range(heads):
        one = query[:, head * head_dim : (head + 1) * head_dim]
        mean = jnp.mean(one * one, axis=1, keepdims=True)
        queries_all[me, head * rows : (head + 1) * rows, :] = (
            one * lax.rsqrt(mean + EPSILON) * q_gain_ref[...].astype(F32)
        ).astype(BF16)

    arrive = gather(queries_all)
    loop(n // 2, lambda i: arrive(2 * i + 1 - core))
    loads[2].wait()
    loads[3].wait()

    factor = head_dim**-0.5 * math.log2(math.e)
    first_block = me * (tokens // BLK)
    chunk = min(2 * rows, heads * rows)

    def attend(block):
        group = (block * heads) // group_size
        columns = pl.ds(pl.multiple_of(group * head_dim, head_dim), head_dim)
        for start in range(0, heads * rows, chunk):
            query_rows = queries_all[block, start : start + chunk, :]
            scores = lax.dot_general(
                query_rows, keys[:, columns], (((1,), (1,)), ((), ())), preferred_element_type=F32
            )
            limit = limits[start : start + chunk, :]
            tiles = [
                jnp.where(
                    limit >= first_block + j, scores[:, j * BLK : (j + 1) * BLK] * factor, -jnp.inf
                )
                for j in range(tokens // BLK)
            ]
            top = functools.reduce(jnp.maximum, tiles)
            top = jnp.maximum(jnp.max(top, axis=1, keepdims=True), -1e30)
            tiles = [jnp.exp2(tile - top) for tile in tiles]
            total = jnp.sum(functools.reduce(jnp.add, tiles), axis=1, keepdims=True)
            weights = jnp.concatenate([tile.astype(BF16) for tile in tiles], axis=1)
            summed = jnp.dot(weights, values[:, columns], preferred_element_type=F32)
            sums[block, start : start + chunk, :] = summed.astype(BF16)
            for inner in range(0, chunk, rows):
                head = (start + inner) // rows
                for row, value in ((head, top), (heads + head, total)):
                    spread = jnp.broadcast_to(value[inner : inner + rows, :], (rows, rows))
                    stats[block, row : row + 1, :] = spread.T[:1, :]

    def merge(block, arrived):
        more_sums, more_stats = arrived
        mine, theirs = stats[block], more_stats[...]
        top = jnp.maximum(mine[:heads], theirs[:heads])
        decay, decay_more = jnp.exp2(mine[:heads] - top), jnp.exp2(theirs[:heads] - top)
        stats[block, :heads, :] = top
        stats[block, heads : 2 * heads, :] = (
            mine[heads : 2 * heads] * decay + theirs[heads : 2 * heads] * decay_more
        )
        for head in range(heads):
            span = slice(head * rows, (head + 1) * rows)
            one = jnp.broadcast_to(decay[head : head + 1, :], (rows, rows)).T
            two = jnp.broadcast_to(decay_more[head : head + 1, :], (rows, rows)).T
            sums[block, span, :] = (
                sums[block, span, :].astype(F32) * one[:, :1]
                + more_sums[span, :].astype(F32) * two[:, :1]
            ).astype(BF16)

    reduce(
        [
            (sums, sums_core, sums_y, sums_up, sums_down),
            (stats, stats_core, stats_y, stats_up, stats_down),
        ],
        attend,
        merge,
    )
    for head in range(heads):
        total = jnp.broadcast_to(stats[me, heads + head : heads + head + 1, :], (rows, rows)).T
        attended[:, head * head_dim : (head + 1) * head_dim] = (
            sums[me, head * rows : (head + 1) * rows, :].astype(F32) / total[:, :1]
        ).astype(BF16)
    loads[4].wait()

    def mix(block):
        columns = pl.ds(pl.multiple_of(block * width, width), width)
        mixed[block] = jnp.dot(
            attended[...], ow[:, columns], preferred_element_type=F32
        ).astype(BF16)

    def total_of(block, arrived):
        mixed[block] = (mixed[block].astype(F32) + arrived[0][...].astype(F32)).astype(BF16)

    reduce([(mixed, mixed_core, mixed_y, mixed_up, mixed_down)], mix, total_of)
    fresh = (first[me, :rows, :].astype(F32) + mixed[me].astype(F32)).astype(BF16)
    hidden_out[...] = fresh
    second[me] = fresh
    arrive = gather(second)
    loads[5].wait()
    next_out[...] = project(second, 1, nw, arrive).astype(BF16)
    for drain in drains:
        drain()


def on_device(
    hidden,
    attn_gain,
    q_weight,
    q_gain,
    key_cache,
    value_cache,
    block_limit,
    out_weight,
    next_gain,
    next_weight,
):
    n = lax.axis_size("ctx")
    depth = n // 4
    rows, width = hidden.shape
    head_dim = q_gain.shape[0]
    heads = width // head_dim
    group_size = heads * n // (key_cache.shape[1] // head_dim)
    block = jnp.concatenate(
        [hidden, attn_gain[None], next_gain[None], jnp.zeros((14, width), hidden.dtype)], axis=0
    )
    tall, lines = heads * rows, max(8, 2 * heads)

    def slots(count):
        return [
            pltpu.VMEM((count, tall, head_dim), BF16),
            pltpu.VMEM((count, lines, rows), F32),
            pltpu.VMEM((count, rows, width), BF16),
        ]

    vmem, hbm = pl.BlockSpec(memory_space=pltpu.VMEM), pl.BlockSpec(memory_space=pl.ANY)
    return pl.pallas_call(
        functools.partial(kernel, n, group_size),
        out_shape=[jax.ShapeDtypeStruct((rows, width), BF16)] * 2,
        in_specs=[vmem] * 3 + [hbm] * 5,
        out_specs=[vmem] * 2,
        scratch_shapes=[
            pltpu.VMEM(q_weight.shape, BF16),
            pltpu.VMEM(key_cache.shape, BF16),
            pltpu.VMEM(value_cache.shape, BF16),
            pltpu.VMEM(out_weight.shape, BF16),
            pltpu.VMEM(next_weight.shape, BF16),
            pltpu.VMEM((n, rows + 16, width), BF16),
            pltpu.VMEM((n, tall, head_dim), BF16),
            pltpu.VMEM((n, rows, width), BF16),
            *slots(n),
            *slots(2 * depth),
            *slots(depth),
            *slots(depth),
            *slots(depth),
            pltpu.VMEM((rows, width), F32),
            pltpu.VMEM((rows, BLK), F32),
            pltpu.VMEM((tall, BLK), jnp.int32),
            pltpu.VMEM((rows, width), BF16),
            pltpu.SemaphoreType.DMA((3 * (n + 5 * depth) + 30 * depth,)),
            pltpu.SemaphoreType.DMA((6,)),
        ],
        compiler_params=pltpu.CompilerParams(
            collective_id=0, has_side_effects=True, vmem_limit_bytes=67043328
        ),
    )(
        block,
        q_gain[None],
        block_limit[:, None],
        q_weight,
        key_cache,
        value_cache,
        out_weight,
        next_weight,
    )


def solution(mesh):
    in_specs = (
        P("groups", "ctx"),
        P("ctx"),
        P(None, "ctx"),
        P(),
        P(("groups", "ctx"), None),
        P(("groups", "ctx"), None),
        P("groups"),
        P("ctx", None),
        P("ctx"),
        P(None, "ctx"),
    )
    out_specs = (P("groups", "ctx"), P("groups", "ctx"))

    def step(*args):
        return tuple(on_device(*args))

    return jax.shard_map(step, mesh=mesh, in_specs=in_specs, out_specs=out_specs, check_vma=False)
```

time: 451 us -> 159 us (0.35)
  blocking collectives: 160 us -> 0 us
  waiting for transfers between devices: 156 us -> 0 us
  Pallas kernels: 0 us -> 151 us
  matrix products: 58.6 us -> 0 us
  other arithmetic: 32 us -> 1.65 us
  loops' own time: 21.1 us -> 0 us
  between operations: 14.6 us -> 0.65 us
    pallas_call x0 -> x1, Pallas kernels: none -> 151 us  [on_device(): pl.pallas_call(functools.partial(kernel, n, group_size), out_shape=[jax.S...]
    all_gather x3 -> x0, waiting for transfers between devices: 83.5 us -> none  [the longest x2 43.1 us: normalize_project(): lax.all_gather(share, 'ctx', axis=1, tiled=True)]
    reduce_scatter x2 -> x0, waiting for transfers between devices: 72.1 us -> none  [the longest x1 71.8 us: on_device(): lax.psum_scatter(lax.dot_general(out_weight, attended, (((0,), (1,)), (()...]
    pmax x1 -> x0, blocking collectives: 59.4 us -> none  [on_device(): decay = jnp.exp(top - lax.pmax(top, 'ctx'))]
    dot_general x19 -> x0, matrix products: 58.6 us -> none  [the longest x8 22.3 us: one_group(): jnp.dot(expo.astype(jnp.bfloat16), values, preferred_element_type=jnp.flo...]
    unnamed x1 -> x0, blocking collectives: 57.8 us -> none
    all_gather x2 -> x0, blocking collectives: 42.5 us -> none  [normalize_project(): lax.all_gather(gain_share, 'ctx', axis=0, tiled=True)]
    reduce_sum x11 -> x0, other arithmetic: 23.7 us -> none  [the longest x8 19.3 us: one_group(): return (sums, top, jnp.sum(expo, axis=1))]
  transfers between devices with their start and end apart: 5 -> 0, of which waited for: 5 -> 0; matrix products, arithmetic and copies ran while one was open for 0% -> 0% of each run, Pallas kernels for 0% -> 0%
where the time goes in v2:
time: 159 us
  Pallas kernels  151 us (95%)
  local copies, waits for them, and re-layouts  5.97 us (4%)
  other arithmetic  1.65 us (1%)
    pallas_call x1, Pallas kernels, on_device(): pl.pallas_call(functools.partial(kernel, n, group_size), out_shape=[jax.S...  151 us

profile of v2, /device:TPU:0, one launch (start us, length us, event | category | flops | bytes accessed | tf_op | source)
XLA Modules:
  0.0 159.0 jit_solution(4077221718270686383)
XLA Ops:
  0.6 0.1 pad.3.clone
  0.7 0.7 broadcast_in_dim.15
  1.4 0.7 broadcast_in_dim.16
  2.1 1.4 copy.12.limit_ref
  3.5 1.6 %maximum_maximum_fusion.block_in = bf16[144,512]{1,0:T(8,128)(2,1)} fusion(bf16[1,512]{1,0:T(2,128)(2,1)S(1)} %broadcast_in_dim.16, bf16[1,512]{1,0:T(2,128)(2,1)S(1)} %broadcast_in_dim.15, bf16[128,512]{1,0:T(8,128)(2,1)} %param.10, bf16[144]{0:T(256)(128)(2,1)S(1)} %pad.3.clone), kind=kLoop, calls=%fused_computation | loop fusion | flops 589824 | bytes 280864 | tf_op jit(solution)/shard_map/concatenate | solution.py:449
  5.1 150.8 %shard_map.113 = (bf16[128,512]{1,0:T(8,128)(2,1)}, bf16[128,512]{1,0:T(8,128)(2,1)}) custom-call(bf16[144,512]{1,0:T(8,128)(2,1)} %maximum_maximum_fusion.block_in, bf16[1,128]{1,0:T(2,128)(2,1)} %bitcast.3, s32[128,1]{1,0:T(8,128)} %copy.12.limit_ref, bf16[8192,512]{1,0:T(8,128)(2,1)} %qw_hbm.1, bf16[1536,1024]{1,0:T(8,128)(2,1)} %key_hbm.1, ...), custom_call_target="tpu_custom_call" | custom-call | tf_op jit(solution)/shard_map/pallas_call | solution.py:462
  155.9 1.6 copy.15
  157.5 1.6 copy.16
  (1 shorter events, 0.0 us)

commit v3 on v2

--- a/solution.py
+++ b/solution.py
@@ -25,7 +25,9 @@
 def kernel(
     n,
     group_size,
-    block_in,
+    hidden_in,
+    attn_gain_ref,
+    next_gain_ref,
     q_gain_ref,
     limit_ref,
     qw_hbm,
@@ -84,7 +86,7 @@
         pltpu.make_async_copy(src, dst, local_sems.at[i])
         for i, (src, dst) in enumerate(
             [
-                (block_in, first.at[me]),
+                (hidden_in, first.at[me, pl.ds(0, rows)]),
                 (qw_hbm, qw),
                 (key_hbm, keys),
                 (value_hbm, values),
@@ -96,6 +98,10 @@
     for load in loads:
         load.start()
 
+    line = lax.broadcasted_iota(jnp.int32, (16, width), 0)
+    gains = [jnp.broadcast_to(g[...].astype(F32), (16, width)) for g in (attn_gain_ref, next_gain_ref)]
+    first[me, rows : rows + 16, :] = jnp.where(line == 0, gains[0], gains[1]).astype(BF16)
+
     barrier = pltpu.get_barrier_semaphore()
 
     def greet(device):
@@ -108,8 +114,18 @@
     peers = 2 + jnp.where(z + 1 < depth, 1, 0) + jnp.where(z > 0, 1, 0)
     pl.semaphore_wait(barrier, peers)
 
+    limit_rows = jnp.broadcast_to(limit_ref[...], (rows, rows)).T[:, :1]
     for head in range(heads):
-        limits[head * rows : (head + 1) * rows, :] = jnp.broadcast_to(limit_ref[...], (rows, BLK))
+        limits[head * rows : (head + 1) * rows, :] = jnp.broadcast_to(limit_rows, (rows, BLK))
+
+    before, after = z, depth - 1 - z
+    lone, paired = jnp.abs(after - before), jnp.minimum(after, before)
+
+    def farthest(i):
+        j = jnp.maximum(i - lone, 0)
+        distance = paired - lax.div(j, 2)
+        near = z + jnp.where(lax.rem(j, 2) == 0, distance, -distance)
+        return jnp.where(i < lone, jnp.where(after > before, depth - 1 - i, i), near)
 
     def remote(src, dst, send, recv, device):
         return pltpu.make_async_remote_copy(
@@ -124,7 +140,7 @@
     used = [0]
     drains = []
 
-    def gather(buffer):
+    def gather(buffer, ready, consume):
         base = used[0]
         used[0] += n + 5 * depth
         send = base + n
@@ -149,14 +165,16 @@
 
         def column(step, sign):
             zz = z + sign * step
-
-            @pl.when((zz >= 0) & (zz < depth))
+            start = step == 0
+            fresh = jnp.logical_not(start) if sign > 0 else step >= 0
+
+            @pl.when((zz >= 0) & (zz < depth) & fresh)
             def _():
-                if step > 0:
-                    arrive(at(zz, y, core))
-                if step == 0 or sign < 0:
+                pl.when(step > 0)(lambda: arrive(at(zz, y, core)))
+                if sign < 0:
                     pl.when(z + 1 < depth)(lambda: to_above(zz).start())
-                if step == 0 or sign > 0:
+                    pl.when(start & (z > 0))(lambda: to_below(zz).start())
+                else:
                     pl.when(z > 0)(lambda: to_below(zz).start())
                 to_y(zz).start()
                 to_core(zz, y).start()
@@ -164,18 +182,31 @@
         def beside(step, sign):
             zz = z + sign * step
 
-            @pl.when((zz >= 0) & (zz < depth))
+            @pl.when((zz >= 0) & (zz < depth) & (step >= (1 if sign > 0 else 0)))
             def _():
                 arrive(at(zz, 1 - y, core))
                 to_core(zz, 1 - y).start()
 
-        for step in range(depth + 1):
-            if step < depth:
-                for sign in (-1, 1) if step else (-1,):
-                    column(step, sign)
-            if step > 0:
-                for sign in (-1, 1) if step > 1 else (-1,):
-                    beside(step - 1, sign)
+        def turn(step):
+            column(step, -1)
+            column(step, 1)
+            beside(step - 1, -1)
+            beside(step - 1, 1)
+            pl.when(step == 1)(ready)
+
+            def use(i):
+                distance = step - 1
+                upward = i >= 2
+                zz = z + jnp.where(upward, distance, -distance)
+                fresh = (distance > 0) | jnp.logical_not(upward)
+
+                @pl.when((distance >= 0) & (zz >= 0) & (zz < depth) & fresh)
+                def _():
+                    consume(at(zz, lax.rem(i, 2), core))
+
+            loop(4, use)
+
+        loop(depth + 1, turn)
 
         def drain():
             def one(zz):
@@ -190,7 +221,7 @@
         drains.append(drain)
         return arrive
 
-    def reduce(arrays, compute, combine):
+    def reduce(arrays, compute_other, compute, combine):
         starts = []
         for _ in arrays:
             starts.append(used[0])
@@ -230,52 +261,51 @@
         def add(block, which, slot):
             combine(block, [array[which].at[slot] for array in arrays])
 
-        def send_core(i):
-            zz, yy = lax.rem(i, depth), jnp.where(i < depth, 1 - y, y)
-            compute(at(zz, yy, 1 - core))
-            begin(0, zz, yy)
-
-        def send_y(zz):
-            block = at(zz, 1 - y, core)
-            compute(block)
-            received(0, zz, 1 - y)
-            add(block, 1, 2 * zz + 1 - y)
-            begin(1, zz)
-
-        def keep(zz):
+        def spread(zz):
+            def across(i):
+                yy = jnp.where(i == 0, 1 - y, y)
+                compute_other(at(zz, yy, 1 - core))
+                begin(0, zz, yy)
+
+            def here(i):
+                yy = jnp.where(i == 0, 1 - y, y)
+                block = at(zz, yy, core)
+                compute(block)
+                received(0, zz, yy)
+                add(block, 1, 2 * zz + yy)
+                pl.when(i == 0)(lambda: begin(1, zz))
+
+            loop(2, across)
+            loop(2, here)
+
+        def along(zz):
             block = at(zz, y, core)
-            compute(block)
-            received(0, zz, y)
-            add(block, 1, 2 * zz + y)
             received(1, zz)
             add(block, 2, zz)
 
-        loop(2 * depth, send_core)
-        loop(depth, send_y)
-        loop(depth, keep)
-
-        def along(k):
-            high, low = depth - 1 - k, k
-
-            @pl.when(high > z)
+            @pl.when(zz > z)
             def _():
                 @pl.when(z > 0)
                 def _():
-                    received(2, high)
-                    add(at(high, y, core), 3, high)
-
-                begin(2, high)
-
-            @pl.when(low < z)
+                    received(2, zz)
+                    add(block, 3, zz)
+
+                begin(2, zz)
+
+            @pl.when(zz < z)
             def _():
                 @pl.when(z + 1 < depth)
                 def _():
-                    received(3, low)
-                    add(at(low, y, core), 4, low)
-
-                begin(3, low)
-
-        loop(depth, along)
+                    received(3, zz)
+                    add(block, 4, zz)
+
+                begin(3, zz)
+
+        def step(i):
+            pl.when(i < depth)(lambda: spread(farthest(i)))
+            pl.when(i > 0)(lambda: along(farthest(i - 1)))
+
+        loop(depth + 1, step)
 
         @pl.when(z > 0)
         def _():
@@ -299,7 +329,7 @@
 
         drains.append(drain)
 
-    def project(buffer, gain_row, weight, arrive):
+    def project(buffer, gain_row, weight, load):
         acc[...] = jnp.zeros_like(acc)
         squares[...] = jnp.zeros_like(squares)
 
@@ -316,7 +346,7 @@
                 (part * gain).astype(BF16), weight[depth_rows, :], preferred_element_type=F32
             )
 
-        loop(n // 2, lambda i: term(2 * i + core))
+        arrive = gather(buffer, load.wait, term)
 
         def last(i):
             block = 2 * i + 1 - core
@@ -328,20 +358,13 @@
         return acc[...] * lax.rsqrt(mean + EPSILON)
 
     loads[0].wait()
-    arrive = gather(first)
-    loads[1].wait()
-    query = project(first, 0, qw, arrive)
+    query = project(first, 0, qw, loads[1])
     for head in range(heads):
         one = query[:, head * head_dim : (head + 1) * head_dim]
         mean = jnp.mean(one * one, axis=1, keepdims=True)
         queries_all[me, head * rows : (head + 1) * rows, :] = (
             one * lax.rsqrt(mean + EPSILON) * q_gain_ref[...].astype(F32)
         ).astype(BF16)
-
-    arrive = gather(queries_all)
-    loop(n // 2, lambda i: arrive(2 * i + 1 - core))
-    loads[2].wait()
-    loads[3].wait()
 
     factor = head_dim**-0.5 * math.log2(math.e)
     first_block = me * (tokens // BLK)
@@ -393,12 +416,23 @@
                 + more_sums[span, :].astype(F32) * two[:, :1]
             ).astype(BF16)
 
+    def caches_ready():
+        loads[2].wait()
+        loads[3].wait()
+
+    arrive = gather(queries_all, caches_ready, attend)
+
+    def attend_late(block):
+        arrive(block)
+        attend(block)
+
     reduce(
         [
             (sums, sums_core, sums_y, sums_up, sums_down),
             (stats, stats_core, stats_y, stats_up, stats_down),
         ],
-        attend,
+        attend_late,
+        lambda block: None,
         merge,
     )
     for head in range(heads):
@@ -417,13 +451,11 @@
     def total_of(block, arrived):
         mixed[block] = (mixed[block].astype(F32) + arrived[0][...].astype(F32)).astype(BF16)
 
-    reduce([(mixed, mixed_core, mixed_y, mixed_up, mixed_down)], mix, total_of)
+    reduce([(mixed, mixed_core, mixed_y, mixed_up, mixed_down)], mix, mix, total_of)
     fresh = (first[me, :rows, :].astype(F32) + mixed[me].astype(F32)).astype(BF16)
     hidden_out[...] = fresh
     second[me] = fresh
-    arrive = gather(second)
-    loads[5].wait()
-    next_out[...] = project(second, 1, nw, arrive).astype(BF16)
+    next_out[...] = project(second, 1, nw, loads[5]).astype(BF16)
     for drain in drains:
         drain()
 
@@ -446,9 +478,6 @@
     head_dim = q_gain.shape[0]
     heads = width // head_dim
     group_size = heads * n // (key_cache.shape[1] // head_dim)
-    block = jnp.concatenate(
-        [hidden, attn_gain[None], next_gain[None], jnp.zeros((14, width), hidden.dtype)], axis=0
-    )
     tall, lines = heads * rows, max(8, 2 * heads)
 
     def slots(count):
@@ -462,7 +491,7 @@
     return pl.pallas_call(
         functools.partial(kernel, n, group_size),
         out_shape=[jax.ShapeDtypeStruct((rows, width), BF16)] * 2,
-        in_specs=[vmem] * 3 + [hbm] * 5,
+        in_specs=[vmem] * 5 + [hbm] * 5,
         out_specs=[vmem] * 2,
         scratch_shapes=[
             pltpu.VMEM(q_weight.shape, BF16),
@@ -489,9 +518,11 @@
             collective_id=0, has_side_effects=True, vmem_limit_bytes=67043328
         ),
     )(
-        block,
+        hidden,
+        attn_gain[None],
+        next_gain[None],
         q_gain[None],
-        block_limit[:, None],
+        block_limit[None],
         q_weight,
         key_cache,
         value_cache,

time: 159 us -> 129 us (0.81)
  Pallas kernels: 151 us -> 123 us
  other arithmetic: 1.65 us -> 0 us
    pallas_call x1, Pallas kernels: 151 us -> 123 us  [on_device(): pl.pallas_call(functools.partial(kernel, n, group_size), out_shape=[jax.S...]
    concatenate x1 -> x0, other arithmetic: 1.65 us -> none  [on_device(): jnp.concatenate([hidden, attn_gain[None], next_gain[None], jnp.zeros((14,...]
where the time goes in v3:
time: 129 us
  Pallas kernels  123 us (95%)
  local copies, waits for them, and re-layouts  5.65 us (4%)
    pallas_call x1, Pallas kernels, on_device(): pl.pallas_call(functools.partial(kernel, n, group_size), out_shape=[jax.S...  123 us
    unnamed x2, local copies, waits for them, and re-layouts  3.14 us

profile of v3, /device:TPU:0, one launch (start us, length us, event | category | flops | bytes accessed | tf_op | source)
XLA Modules:
  0.0 128.9 jit_solution(16425636754994460016)
XLA Ops:
  0.6 1.3 broadcast_in_dim.12.attn_gain_ref
  1.9 1.3 broadcast_in_dim.13.next_gain_ref
  3.1 122.6 %shard_map.113 = (bf16[128,512]{1,0:T(8,128)(2,1)}, bf16[128,512]{1,0:T(8,128)(2,1)}) custom-call(bf16[128,512]{1,0:T(8,128)(2,1)} %hidden_in.1, bf16[1,512]{1,0:T(2,128)(2,1)} %broadcast_in_dim.12.attn_gain_ref, bf16[1,512]{1,0:T(2,128)(2,1)} %broadcast_in_dim.13.next_gain_ref, bf16[1,128]{1,0:T(2,128)(2,1)} %bitcast.2, s32[1,128]{1,0:T(1,128)} %bitcast.3, ...), custom_call_target="tpu_custom_call" | custom-call | tf_op jit(solution)/shard_map/pallas_call | solution.py:491
  125.7 1.6 %copy.14 = bf16[128,512]{1,0:T(8,128)(2,1)} copy(bf16[128,512]{1,0:T(8,128)(2,1)} %get-tuple-element.4) | data formatting | bytes 262144
  127.3 1.6 %copy.15 = bf16[128,512]{1,0:T(8,128)(2,1)} copy(bf16[128,512]{1,0:T(8,128)(2,1)} %get-tuple-element.5) | data formatting | bytes 262144
